TPU v7x, 32 devices: a whole 2x2x4 slice. The times are simulated.
32 devices in a mesh: member: 4 (over y, x), slab: 8 (over z, core).
Axes of the slice: x: 2, y: 2, z: 4, core: 2. Of those that a mesh axis runs over, the one named last changes fastest.
Arguments:
- control: float32 [16, 2, 1024, 2048], P('member', None, 'slab'), may hold values from -6 to 6
- perturbation: bfloat16 [16, 2, 1024, 2048], P('member', None, 'slab'), may hold values from -6 to 6
- loc_row: float32 [2, 1024], P(None, 'slab'), may hold values from 0.2 to 2
- loc_col: float32 [2, 2048], replicated, may hold values from 0.2 to 2
- obs_tile: int32 [2048], P('slab'), may hold values from 0 to 4095, as said below
- obs_count: int32 [2048], P('slab'), may hold values from 1 to 128
- obs_value: float32 [2048, 128], P('slab'), may hold values from -12 to 12
Outputs:
- gradient: float32 [16, 2, 1024, 2048], P('member', None, 'slab')
Inputs may be any that keep to these rules, and one draw needn't show every extreme that they name: `obs_tile`: entry i names a tile of slab block i // 256 in that block's numbering, whose columns lie in column share k = (i mod 256) // (256 / 8), i.e. columns k * 2048 / 8 onward; tiles may repeat. cells 0 to obs_count - 1 of a tile are observed.
All inputs are finite; a program needn't handle non-finite values.
Results may differ from a plain program's by a relative error of at most 0.012.
Values may be sent and summed in bfloat16 or wider, within the bound.
A program may use at most 64 MiB of HBM per device.

v0:
```python
import jax
import jax.numpy as jnp
from jax import lax
from jax.sharding import PartitionSpec as P

TILE = 128


def hartley(order):
    index = jnp.arange(order, dtype=jnp.int32)
    product = index[:, None] * index[None, :] % order
    angle = 2.0 * jnp.pi * product.astype(jnp.float32) / order
    table = (jnp.cos(angle) + jnp.sin(angle)) / jnp.sqrt(jnp.float32(order))
    return table.astype(jnp.bfloat16)


def shards(control, perturbation, loc_row, loc_col, obs_tile, obs_count, obs_value):
    members, levels, rows, width = control.shape
    slabs = lax.axis_size("slab")
    height = rows * slabs
    share = width // slabs
    table_y = hartley(height)
    table_x = hartley(width)
    amplitude = loc_row[:, :, None] * loc_col[:, None, :]

    def columns_pass(block):
        product = jnp.einsum("ya,mlac->mlyc", table_y, block, preferred_element_type=jnp.float32)
        return product.astype(jnp.bfloat16)

    scaled = (control * amplitude[None]).astype(jnp.bfloat16)
    along = jnp.dot(scaled.reshape(-1, width), table_x, preferred_element_type=jnp.float32)
    along = along.astype(jnp.bfloat16).reshape(members, levels, rows, width)
    field_cols = columns_pass(
        lax.all_to_all(along, "slab", split_axis=3, concat_axis=2, tiled=True)
    )
    tile_total = levels * rows * (width // TILE)
    all_tiles = lax.all_gather(obs_tile, "slab", axis=0, tiled=True)
    per_peer = obs_tile.shape[0] // slabs
    mine = lax.axis_index("slab")
    listed = lax.dynamic_slice_in_dim(all_tiles.reshape(slabs, slabs, per_peer), mine, 1, 1)
    listed = listed.reshape(slabs, per_peer)
    per_row = width // TILE
    level = listed // (rows * per_row)
    row_in = listed // per_row % rows
    local_tile = listed % per_row - mine * (share // TILE)
    source = jnp.arange(slabs, dtype=jnp.int32)[:, None]
    flat_index = ((level * height + source * rows + row_in) * (share // TILE) + local_tile).reshape(
        -1
    )
    picked = field_cols.reshape(members, -1, TILE)[:, flat_index]
    field_obs = lax.all_to_all(picked, "slab", split_axis=1, concat_axis=1, tiled=True)
    pert_obs = perturbation.reshape(members, -1, TILE)[:, obs_tile].astype(jnp.float32)
    partial_obs = jnp.sum(pert_obs * field_obs.astype(jnp.float32), axis=0)
    cells = lax.psum(partial_obs, "member")
    resid = cells - obs_value
    observed = jnp.arange(TILE, dtype=jnp.int32)[None, :] < obs_count[:, None]
    score = jnp.where(observed, resid / jnp.sqrt(1.0 + resid * resid / 4.0), 0.0)
    adjoint_tiles = jnp.zeros((tile_total, TILE), jnp.float32).at[obs_tile].add(score)
    weighted_obs = (pert_obs * adjoint_tiles[obs_tile][None]).astype(jnp.bfloat16)
    arrived = lax.all_to_all(weighted_obs, "slab", split_axis=1, concat_axis=1, tiled=True)
    empty = jnp.zeros((members, levels * height * (share // TILE), TILE), jnp.bfloat16)
    filled = empty.at[:, flat_index].set(arrived)
    back_cols = columns_pass(filled.reshape(members, levels, height, share))
    back = lax.all_to_all(back_cols, "slab", split_axis=2, concat_axis=3, tiled=True)
    result = jnp.dot(back.reshape(-1, width), table_x, preferred_element_type=jnp.float32)
    return result.reshape(members, levels, rows, width) * amplitude[None]


def solution(mesh):
    placed = (
        P("member", None, "slab", None),
        P("member", None, "slab", None),
        P(None, "slab"),
        P(),
        P("slab"),
        P("slab"),
        P("slab", None),
    )
    return jax.shard_map(
        shards,
        mesh=mesh,
        in_specs=placed,
        out_specs=P("member", None, "slab", None),
        check_vma=False,
    )
```

profile of v0, /device:TPU:0, one launch (start us, length us, event | category | flops | bytes accessed | tf_op | source)
XLA Modules:
  0.0 563.9 jit_solution(10304791134085167966)
XLA Ops:
  6.5 0.0 copy-start.2
  6.5 0.0 copy-start.5
  6.5 0.0 copy-start
  6.5 68.2 %multiply_convert_fusion.9 = bf16[2048,2048]{1,0:T(8,128)(2,1)} fusion(), kind=kLoop, calls=%fused_computation.11.clone.1.clone.clone.clone.1 | loop fusion | flops 71303168 | bytes 8388608 | tf_op jit(solution)/shard_map/dot_general | solution.py:31
  74.7 0.0 copy-done.2
  74.7 0.0 copy-done.5
  74.7 0.2 broadcast_multiply_fusion
  74.9 0.0 copy-done
  74.9 1.4 multiply_convert_fusion.3
  76.4 12.6 %fusion.18 = bf16[1024,2048]{1,0:T(8,128)(2,1)} fusion(bf16[1024,2048]{1,0:T(8,128)(2,1)S(1)} %bitcast.61, bf16[2048,2048]{1,0:T(8,128)(2,1)} %multiply_convert_fusion.9), kind=kOutput, calls=%fused_computation.34 | convolution fusion | flops 8592031744 | bytes 16777216 | tf_op jit(solution)/shard_map/dot_general | solution.py:31
  89.0 11.1 %copy.24 = bf16[4,2,128,2048]{2,1,0,3:T(2,128)(2,1)} copy(bf16[4,2,128,2048]{3,2,1,0:T(8,128)(2,1)} %bitcast.62) | data formatting | bytes 8388608 | tf_op jit(solution)/shard_map/reshape | solution.py:32
  100.1 0.0 copy-start.3
  100.1 6.5 %all-to-all-start = ((bf16[4,2,128,2048]{2,1,0,3:T(2,128)(2,1)}), bf16[4,2,128,2048]{2,1,0,3:T(2,128)(2,1)}, u32[]{:S(2)}, u32[]{:S(2)}) async-start(bf16[4,2,128,2048]{2,1,0,3:T(2,128)(2,1)} %copy.24), calls=%async_computation | async-start | bytes 8388608 | tf_op jit(solution)/shard_map/all_to_all | solution.py:34
  106.6 0.0 copy-done.3
  106.6 75.3 %all-gather = s32[8,1,256]{2,1,0:T(1,128)S(1)} all-gather(s32[1,1,256]{2,1,0:T(1,128)S(1)} %bitcast.66), channel_id=1, replica_groups=mesh['member'=4,'slab'=8] {'slab'}, dimensions={0}, use_global_device_ids=true | all-gather | bytes 9216 | tf_op jit(solution)/shard_map/all_gather | solution.py:37
  181.9 0.1 reshape.231
  182.0 0.1 reshape.232
  182.1 0.1 add.140
  182.1 0.1 add.141
  182.3 18.5 %all-to-all-done = bf16[4,2,128,2048]{2,1,0,3:T(2,128)(2,1)} async-done(((bf16[4,2,128,2048]{2,1,0,3:T(2,128)(2,1)}), bf16[4,2,128,2048]{2,1,0,3:T(2,128)(2,1)}, u32[]{:S(2)}, u32[]{:S(2)}) %all-to-all-start) | async-done | bytes 4194336 | tf_op jit(solution)/shard_map/all_to_all | solution.py:34
  200.7 6.9 %copy.38 = bf16[4,2,128,8,256]{2,3,4,1,0:T(8,128)(2,1)} copy(bf16[4,2,128,8,256]{2,1,0,4,3:T(2,128)(2,1)} %bitcast.5) | data formatting | bytes 8388608 | tf_op jit(solution)/shard_map/all_to_all | solution.py:34
  207.6 7.3 %all_to_all.33 = bf16[4,2,1024,256]{2,3,1,0:T(8,128)(2,1)} reshape(bf16[4,2,8,128,256]{3,2,4,1,0:T(8,128)(2,1)} %bitcast.59) | data formatting | bytes 8388608 | tf_op jit(solution)/shard_map/all_to_all | solution.py:34
  214.9 23.3 %convert_bitcast_fusion.1 = bf16[4,2,1024,256]{2,3,1,0:T(8,128)(2,1)} fusion(bf16[4,2,1024,256]{2,3,1,0:T(8,128)(2,1)} %all_to_all.33), kind=kOutput, calls=%fused_computation.29 | convolution fusion | flops 4314890240 | bytes 8388608 | tf_op jit(solution)/shard_map/ya,mlac->mlyc/dot_general | solution.py:27
  238.2 6.2 %copy.26 = bf16[4,2,1024,256]{3,2,1,0:T(8,128)(2,1)} copy(bf16[4,2,1024,256]{2,3,1,0:T(8,128)(2,1)} %convert_bitcast_fusion.1) | data formatting | bytes 8388608 | tf_op jit(solution)/shard_map/convert_element_type | solution.py:28
  244.4 7.1 %reshape.236 = bf16[4,4096,128]{2,1,0:T(8,128)(2,1)} reshape(bf16[4,2,1024,256]{3,2,1,0:T(8,128)(2,1)} %copy.26) | data formatting | bytes 8388608 | tf_op jit(solution)/shard_map/reshape | solution.py:50
  251.5 7.6 %copy.27 = bf16[4,4096,128]{2,0,1:T(4,128)(2,1)} copy(bf16[4,4096,128]{2,1,0:T(8,128)(2,1)} %reshape.236) | data formatting | bytes 8388608 | tf_op jit(solution)/shard_map/reshape | solution.py:50
  259.1 3.8 gather_fusion.1
  262.9 6.0 %all-to-all-start.1 = ((bf16[4,256,128]{2,0,1:T(4,128)(2,1)}), bf16[4,256,128]{2,0,1:T(4,128)(2,1)S(1)}, u32[]{:S(2)}, u32[]{:S(2)}) async-start(bf16[4,256,128]{2,0,1:T(4,128)(2,1)} %bitcast.10), calls=%async_computation.1 | async-start | bytes 524288 | tf_op jit(solution)/shard_map/all_to_all | solution.py:51
  268.9 0.2 all-reduce.2.cloned.1.call-start
  269.1 7.4 %reshape.233 = bf16[4,4096,128]{2,1,0:T(8,128)(2,1)} reshape(bf16[4,2,128,2048]{3,2,1,0:T(8,128)(2,1)} %param.8) | data formatting | bytes 8388608 | tf_op jit(solution)/shard_map/reshape | solution.py:52
  276.5 0.0 copy-start.1
  276.5 0.0 copy-start.4
  276.5 7.6 %copy.23 = bf16[4,4096,128]{2,0,1:T(4,128)(2,1)} copy(bf16[4,4096,128]{2,1,0:T(8,128)(2,1)} %reshape.233) | data formatting | bytes 8388608 | tf_op jit(solution)/shard_map/reshape | solution.py:52
  284.1 3.2 gather_fusion
  287.3 0.0 all-to-all-done.1
  287.3 1.0 fusion.30
  288.4 0.0 all-reduce.2.cloned.1.call-update
  288.4 43.8 %all-reduce.2.cloned.1.call-done = f32[256,128]{1,0:T(8,128)} async-done(((f32[256,128]{1,0:T(8,128)}), f32[256,128]{1,0:T(8,128)}) %all-reduce.2.cloned.1.call-update) | async-done | bytes 131088 | tf_op jit(solution)/shard_map/psum | solution.py:54
  332.2 0.0 copy-done.1
  332.2 0.0 copy-done.4
  332.2 3.3 scatter_custom_fusion
  335.5 2.3 gather_fusion.2
  337.8 0.1 fusion.31
  337.9 14.1 %all_to_all.43 = bf16[4,256,128]{2,0,1:T(4,128)(2,1)S(1)} all-to-all(bf16[4,256,128]{2,0,1:T(4,128)(2,1)S(1)} %fusion.31), channel_id=1, replica_groups=mesh['member'=4,'slab'=8] {'slab'}, dimensions={1} | all-to-all | bytes 524288 | tf_op jit(solution)/shard_map/all_to_all | solution.py:60
  352.0 2.8 broadcast_in_dim.9
  354.9 28.1 %scatter_fusion = bf16[4,4096,128]{2,0,1:T(4,128)(2,1)} fusion(bf16[4,4096,128]{2,0,1:T(4,128)(2,1)} %broadcast_in_dim.9, s32[256]{0:T(256)S(1)} %bitcast.65, bf16[256,4,128]{2,1,0:T(4,128)(2,1)S(1)} %bitcast.63), kind=kCustom, calls=%fused_computation.4 | custom fusion | bytes 787456 | tf_op jit(solution)/shard_map/scatter | solution.py:62
  382.9 4.7 copy.28
  387.6 7.1 %reshape.237 = bf16[4,2,1024,256]{3,2,1,0:T(8,128)(2,1)} reshape(bf16[4,4096,128]{2,1,0:T(8,128)(2,1)} %copy.28) | data formatting | bytes 8388608 | tf_op jit(solution)/shard_map/reshape | solution.py:63
  394.7 23.8 %convert_bitcast_fusion = bf16[4,2,1024,256]{2,3,1,0:T(8,128)(2,1)} fusion(bf16[4,2,1024,256]{3,2,1,0:T(8,128)(2,1)} %reshape.237), kind=kOutput, calls=%fused_computation.28 | convolution fusion | flops 4314890240 | bytes 8388608 | tf_op jit(solution)/shard_map/ya,mlac->mlyc/dot_general | solution.py:27
  418.4 11.1 %copy.30 = bf16[4,2,1024,256]{3,1,0,2:T(2,128)(2,1)} copy(bf16[4,2,1024,256]{2,3,1,0:T(8,128)(2,1)} %convert_bitcast_fusion) | data formatting | bytes 8388608 | tf_op jit(solution)/shard_map/convert_element_type | solution.py:28
  429.6 4.8 all-to-all-start.3
  434.4 68.2 %fusion.75 = bf16[2048,2048,1,1]{1,0,3,2:T(8,128)(2,1)} fusion(), kind=kLoop, calls=%fused_computation.16.clone.clone.clone.1 | loop fusion | flops 71303168 | bytes 8388608 | tf_op jit(solution)/shard_map/dot_general | solution.py:65
  502.6 25.8 %all-to-all-done.3 = bf16[4,2,1024,256]{3,1,0,2:T(2,128)(2,1)} async-done(((bf16[4,2,1024,256]{3,1,0,2:T(2,128)(2,1)}), bf16[4,2,1024,256]{3,1,0,2:T(2,128)(2,1)}, u32[]{:S(2)}, u32[]{:S(2)}) %all-to-all-start.3) | async-done | bytes 4194336 | tf_op jit(solution)/shard_map/all_to_all | solution.py:64
  528.4 6.6 %copy.37 = bf16[4,2,8,128,256]{4,2,3,1,0:T(8,128)(2,1)} copy(bf16[4,2,8,128,256]{4,1,0,3,2:T(2,128)(2,1)} %bitcast.13) | data formatting | bytes 8388608 | tf_op jit(solution)/shard_map/all_to_all | solution.py:64
  534.9 7.4 %dot_general.17 = bf16[4,2,128,2048]{3,2,1,0:T(8,128)(2,1)} reshape(bf16[4,2,128,8,256]{4,3,2,1,0:T(8,128)(2,1)} %bitcast.60) | data formatting | bytes 8388608 | tf_op jit(solution)/shard_map/dot_general | solution.py:65
  542.3 14.5 %fusion.9 = f32[4,2,128,2048]{3,2,1,0:T(8,128)} fusion(bf16[4,2,128,2048]{3,2,1,0:T(8,128)(2,1)} %dot_general.17, f32[2,128,2048]{2,1,0:T(8,128)S(1)} %broadcast_multiply_fusion, bf16[2048,2048,1,1]{1,0,3,2:T(8,128)(2,1)} %fusion.75), kind=kOutput, calls=%fused_computation.22 | convolution fusion | flops 8592031744 | bytes 23068672 | tf_op jit(solution)/shard_map/dot_general | solution.py:65
  (7 shorter events, 0.1 us)
Async XLA Ops:
  6.5 68.2 %copy-start.2 = (f32[2,2048]{1,0:T(2,128)S(1)}, f32[2,2048]{1,0:T(2,128)}, u32[]{:S(2)}) copy-start(f32[2,2048]{1,0:T(2,128)} %param.10) | copy-start | bytes 49156
  6.5 68.2 %copy-start.5 = (f32[2,128]{1,0:T(2,128)S(1)}, f32[2,128]{1,0:T(2,128)}, u32[]{:S(2)}) copy-start(f32[2,128]{1,0:T(2,128)} %param.9) | copy-start | bytes 3076
  6.5 68.4 %copy-start = (f32[4,2,128,2048]{3,2,1,0:T(8,128)S(1)}, f32[4,2,128,2048]{3,2,1,0:T(8,128)}, u32[]{:S(2)}) copy-start(f32[4,2,128,2048]{3,2,1,0:T(8,128)} %param.7) | copy-start | bytes 25165828
  100.1 6.5 %copy-start.3 = (s32[256]{0:T(256)S(1)}, s32[256]{0:T(256)}, u32[]{:S(2)}) copy-start(s32[256]{0:T(256)} %param.11) | copy-start | bytes 3076
  100.1 100.6 %all-to-all-start = ((bf16[4,2,128,2048]{2,1,0,3:T(2,128)(2,1)}), bf16[4,2,128,2048]{2,1,0,3:T(2,128)(2,1)}, u32[]{:S(2)}, u32[]{:S(2)}) async-start(bf16[4,2,128,2048]{2,1,0,3:T(2,128)(2,1)} %copy.24), calls=%async_computation | async-start | bytes 8388608 | tf_op jit(solution)/shard_map/all_to_all | solution.py:34
  262.9 24.4 %all-to-all-start.1 = ((bf16[4,256,128]{2,0,1:T(4,128)(2,1)}), bf16[4,256,128]{2,0,1:T(4,128)(2,1)S(1)}, u32[]{:S(2)}, u32[]{:S(2)}) async-start(bf16[4,256,128]{2,0,1:T(4,128)(2,1)} %bitcast.10), calls=%async_computation.1 | async-start | bytes 524288 | tf_op jit(solution)/shard_map/all_to_all | solution.py:51
  268.9 63.3 %all-reduce.2.cloned.1.call-start = ((), (), s32[]{:S(2)}) async-start(), calls=%async_computation.4 | async-start | bytes 262144 | tf_op jit(solution)/shard_map/psum | solution.py:54
  276.5 55.7 %copy-start.1 = (f32[256,128]{1,0:T(8,128)S(1)}, f32[256,128]{1,0:T(8,128)}, u32[]{:S(2)}) copy-start(f32[256,128]{1,0:T(8,128)} %param.13) | copy-start | bytes 393220
  276.5 55.7 %copy-start.4 = (s32[256]{0:T(256)S(1)}, s32[256]{0:T(256)}, u32[]{:S(2)}) copy-start(s32[256]{0:T(256)} %param.12) | copy-start | bytes 3076
  429.6 98.8 %all-to-all-start.3 = ((bf16[4,2,1024,256]{3,1,0,2:T(2,128)(2,1)}), bf16[4,2,1024,256]{3,1,0,2:T(2,128)(2,1)}, u32[]{:S(2)}, u32[]{:S(2)}) async-start(bf16[4,2,1024,256]{3,1,0,2:T(2,128)(2,1)} %copy.30), calls=%async_computation.3 | async-start | bytes 8388608 | tf_op jit(solution)/shard_map/all_to_all | solution.py:64
Sparse Core Ops, SparseCore 0:
  288.5 43.6 all-reduce.1
where the time goes:
time: 572 us; the launch traced here: 564 us
  other arithmetic  142 us (25%)
  local copies, waits for them, and re-layouts  139 us (24%)
  blocking collectives  89.4 us (16%)
  waiting for transfers between devices  88.1 us (15%)
  matrix products  74.1 us (13%)
  starting transfers between devices  17.5 us (3%)
  between operations  13.7 us (2%)
    all_gather x1, blocking collectives, shards(): all_tiles = lax.all_gather(obs_tile, 'slab', axis=0, tiled=True)  75.3 us
    dot_general x1, other arithmetic, shards(): jnp.dot(back.reshape(-1, width), table_x, preferred_element_type=jnp.floa...  68.2 us
    dot_general x1, other arithmetic, shards(): jnp.dot(scaled.reshape(-1, width), table_x, preferred_element_type=jnp.fl...  68.2 us
    dot_general x2, matrix products, columns_pass(): jnp.einsum('ya,mlac->mlyc', table_y, block, preferred_element_type=jnp.fl...  47.1 us
    psum x1, waiting for transfers between devices, shards(): cells = lax.psum(partial_obs, 'member')  43.8 us
    scatter x2, local copies, waits for them, and re-layouts, shards(): filled = empty.at[:, flat_index].set(arrived)  32.7 us
    all_to_all x1, waiting for transfers between devices, shards(): lax.all_to_all(back_cols, 'slab', split_axis=2, concat_axis=3, tiled=True)  25.8 us
    all_to_all x1, waiting for transfers between devices, shards(): lax.all_to_all(along, 'slab', split_axis=3, concat_axis=2, tiled=True)  18.5 us
  transfers between devices with their start and end apart: 4, of which 3 were waited for; matrix products, arithmetic and copies ran while one was open for 15% of the time, Pallas kernels for 0%

commit v1 on v0

--- a/solution.py
+++ b/solution.py
@@ -51,7 +51,7 @@
     field_obs = lax.all_to_all(picked, "slab", split_axis=1, concat_axis=1, tiled=True)
     pert_obs = perturbation.reshape(members, -1, TILE)[:, obs_tile].astype(jnp.float32)
     partial_obs = jnp.sum(pert_obs * field_obs.astype(jnp.float32), axis=0)
-    cells = lax.psum(partial_obs, "member")
+    cells = jnp.sum(lax.all_gather(partial_obs, "member"), axis=0)
     resid = cells - obs_value
     observed = jnp.arange(TILE, dtype=jnp.int32)[None, :] < obs_count[:, None]
     score = jnp.where(observed, resid / jnp.sqrt(1.0 + resid * resid / 4.0), 0.0)

time: 572 us -> 524 us (0.916)
  waiting for transfers between devices: 88.1 us -> 44.3 us
  between operations: 13.7 us -> 0.36 us
  blocking collectives: 89.4 us -> 99.9 us
    psum x1 -> x0, waiting for transfers between devices: 43.8 us -> none  [shards(): cells = lax.psum(partial_obs, 'member')]
    all_gather x0 -> x1, blocking collectives: none -> 10.6 us  [shards(): cells = jnp.sum(lax.all_gather(partial_obs, 'member'), axis=0)]
  transfers between devices with their start and end apart: 4 -> 3, of which waited for: 3 -> 2; matrix products, arithmetic and copies ran while one was open for 15% -> 17% of each run, Pallas kernels for 0% -> 0%
where the time goes in v1:
time: 524 us; the launch traced here: 516 us
  other arithmetic  141 us (27%)
  local copies, waits for them, and re-layouts  139 us (27%)
  blocking collectives  99.9 us (19%)
  matrix products  74.1 us (14%)
  waiting for transfers between devices  44.3 us (8%)
  starting transfers between devices  17.5 us (3%)
    all_gather x1, blocking collectives, shards(): all_tiles = lax.all_gather(obs_tile, 'slab', axis=0, tiled=True)  75.3 us
    dot_general x1, other arithmetic, shards(): jnp.dot(back.reshape(-1, width), table_x, preferred_element_type=jnp.floa...  68.2 us
    dot_general x1, other arithmetic, shards(): jnp.dot(scaled.reshape(-1, width), table_x, preferred_element_type=jnp.fl...  68.2 us
    dot_general x2, matrix products, columns_pass(): jnp.einsum('ya,mlac->mlyc', table_y, block, preferred_element_type=jnp.fl...  47 us
    scatter x2, local copies, waits for them, and re-layouts, shards(): filled = empty.at[:, flat_index].set(arrived)  32.7 us
    all_to_all x1, waiting for transfers between devices, shards(): lax.all_to_all(back_cols, 'slab', split_axis=2, concat_axis=3, tiled=True)  25.8 us
    all_to_all x1, waiting for transfers between devices, shards(): lax.all_to_all(along, 'slab', split_axis=3, concat_axis=2, tiled=True)  18.5 us
    convert_element_type x2, local copies, waits for them, and re-layouts, columns_pass(): return product.astype(jnp.bfloat16)  17.3 us
  transfers between devices with their start and end apart: 3, of which 2 were waited for; matrix products, arithmetic and copies ran while one was open for 17% of the time, Pallas kernels for 0%

profile of v1, /device:TPU:0, one launch (start us, length us, event | category | flops | bytes accessed | tf_op | source)
XLA Modules:
  0.0 516.3 jit_solution(4024231199536054857)
XLA Ops:
  0.0 0.0 copy-start.2
  0.0 0.0 copy-start.5
  0.0 0.0 copy-start
  0.0 68.2 %multiply_convert_fusion.9 = bf16[2048,2048]{1,0:T(8,128)(2,1)} fusion(), kind=kLoop, calls=%fused_computation.11.clone.1.clone.clone.clone.1 | loop fusion | flops 71303168 | bytes 8388608 | tf_op jit(solution)/shard_map/dot_general | solution.py:31
  68.2 0.0 copy-done.2
  68.2 0.0 copy-done.5
  68.2 0.2 broadcast_multiply_fusion
  68.4 0.0 copy-done
  68.4 1.4 multiply_convert_fusion.3
  69.8 12.6 %fusion.18 = bf16[1024,2048]{1,0:T(8,128)(2,1)} fusion(bf16[1024,2048]{1,0:T(8,128)(2,1)S(1)} %bitcast.62, bf16[2048,2048]{1,0:T(8,128)(2,1)} %multiply_convert_fusion.9), kind=kOutput, calls=%fused_computation.34 | convolution fusion | flops 8592031744 | bytes 16777216 | tf_op jit(solution)/shard_map/dot_general | solution.py:31
  82.4 11.1 %copy.33 = bf16[4,2,128,2048]{2,1,0,3:T(2,128)(2,1)} copy(bf16[4,2,128,2048]{3,2,1,0:T(8,128)(2,1)} %bitcast.63) | data formatting | bytes 8388608 | tf_op jit(solution)/shard_map/reshape | solution.py:32
  93.6 0.0 copy-start.3
  93.6 6.5 %all-to-all-start = ((bf16[4,2,128,2048]{2,1,0,3:T(2,128)(2,1)}), bf16[4,2,128,2048]{2,1,0,3:T(2,128)(2,1)}, u32[]{:S(2)}, u32[]{:S(2)}) async-start(bf16[4,2,128,2048]{2,1,0,3:T(2,128)(2,1)} %copy.33), calls=%async_computation | async-start | bytes 8388608 | tf_op jit(solution)/shard_map/all_to_all | solution.py:34
  100.1 0.0 copy-done.3
  100.1 75.3 %all-gather.1 = s32[8,1,256]{2,1,0:T(1,128)S(1)} all-gather(s32[1,1,256]{2,1,0:T(1,128)S(1)} %bitcast.68), channel_id=1, replica_groups=mesh['member'=4,'slab'=8] {'slab'}, dimensions={0}, use_global_device_ids=true | all-gather | bytes 9216 | tf_op jit(solution)/shard_map/all_gather | solution.py:37
  175.4 0.1 reshape.231
  175.5 0.1 reshape.232
  175.5 0.1 add.138
  175.6 0.1 add.139
  175.7 18.5 %all-to-all-done = bf16[4,2,128,2048]{2,1,0,3:T(2,128)(2,1)} async-done(((bf16[4,2,128,2048]{2,1,0,3:T(2,128)(2,1)}), bf16[4,2,128,2048]{2,1,0,3:T(2,128)(2,1)}, u32[]{:S(2)}, u32[]{:S(2)}) %all-to-all-start) | async-done | bytes 4194336 | tf_op jit(solution)/shard_map/all_to_all | solution.py:34
  194.2 6.9 %copy.47 = bf16[4,2,128,8,256]{2,3,4,1,0:T(8,128)(2,1)} copy(bf16[4,2,128,8,256]{2,1,0,4,3:T(2,128)(2,1)} %bitcast.5) | data formatting | bytes 8388608 | tf_op jit(solution)/shard_map/all_to_all | solution.py:34
  201.1 7.3 %all_to_all.33 = bf16[4,2,1024,256]{2,3,1,0:T(8,128)(2,1)} reshape(bf16[4,2,8,128,256]{3,2,4,1,0:T(8,128)(2,1)} %bitcast.60) | data formatting | bytes 8388608 | tf_op jit(solution)/shard_map/all_to_all | solution.py:34
  208.4 23.3 %convert_bitcast_fusion.1 = bf16[4,2,1024,256]{2,3,1,0:T(8,128)(2,1)} fusion(bf16[4,2,1024,256]{2,3,1,0:T(8,128)(2,1)} %all_to_all.33), kind=kOutput, calls=%fused_computation.29 | convolution fusion | flops 4314890240 | bytes 8388608 | tf_op jit(solution)/shard_map/ya,mlac->mlyc/dot_general | solution.py:27
  231.7 6.2 %copy.35 = bf16[4,2,1024,256]{3,2,1,0:T(8,128)(2,1)} copy(bf16[4,2,1024,256]{2,3,1,0:T(8,128)(2,1)} %convert_bitcast_fusion.1) | data formatting | bytes 8388608 | tf_op jit(solution)/shard_map/convert_element_type | solution.py:28
  237.9 7.1 %reshape.236 = bf16[4,4096,128]{2,1,0:T(8,128)(2,1)} reshape(bf16[4,2,1024,256]{3,2,1,0:T(8,128)(2,1)} %copy.35) | data formatting | bytes 8388608 | tf_op jit(solution)/shard_map/reshape | solution.py:50
  245.0 7.6 %copy.36 = bf16[4,4096,128]{2,0,1:T(4,128)(2,1)} copy(bf16[4,4096,128]{2,1,0:T(8,128)(2,1)} %reshape.236) | data formatting | bytes 8388608 | tf_op jit(solution)/shard_map/reshape | solution.py:50
  252.5 3.8 gather_fusion.1
  256.4 6.2 %all-to-all-start.1 = ((bf16[4,256,128]{2,0,1:T(4,128)(2,1)}), bf16[4,256,128]{2,0,1:T(4,128)(2,1)S(1)}, u32[]{:S(2)}, u32[]{:S(2)}) async-start(bf16[4,256,128]{2,0,1:T(4,128)(2,1)} %bitcast.10), calls=%async_computation.1 | async-start | bytes 524288 | tf_op jit(solution)/shard_map/all_to_all | solution.py:51
  262.6 7.4 %reshape.233 = bf16[4,4096,128]{2,1,0:T(8,128)(2,1)} reshape(bf16[4,2,128,2048]{3,2,1,0:T(8,128)(2,1)} %param.8) | data formatting | bytes 8388608 | tf_op jit(solution)/shard_map/reshape | solution.py:52
  270.0 0.0 copy-start.1
  270.0 0.0 copy-start.4
  270.0 7.6 %copy.32 = bf16[4,4096,128]{2,0,1:T(4,128)(2,1)} copy(bf16[4,4096,128]{2,1,0:T(8,128)(2,1)} %reshape.233) | data formatting | bytes 8388608 | tf_op jit(solution)/shard_map/reshape | solution.py:52
  277.6 3.2 gather_fusion
  280.8 0.0 all-to-all-done.1
  280.8 0.4 fusion.30
  281.2 10.6 %all-gather = f32[1024,128]{1,0:T(8,128)S(1)} all-gather(f32[256,128]{1,0:T(8,128)S(1)} %fusion.30), channel_id=2, replica_groups=mesh['member'=4,'slab'=8] {'member'}, dimensions={0}, use_global_device_ids=true | all-gather | bytes 655360 | tf_op jit(solution)/shard_map/all_gather | solution.py:54
  291.9 0.0 copy-done.1
  291.9 0.0 copy-done.4
  291.9 2.9 scatter_custom_fusion
  294.8 2.3 gather_fusion.2
  297.1 0.1 fusion.31
  297.2 14.0 %all_to_all.43 = bf16[4,256,128]{2,0,1:T(4,128)(2,1)S(1)} all-to-all(bf16[4,256,128]{2,0,1:T(4,128)(2,1)S(1)} %fusion.31), channel_id=1, replica_groups=mesh['member'=4,'slab'=8] {'slab'}, dimensions={1} | all-to-all | bytes 524288 | tf_op jit(solution)/shard_map/all_to_all | solution.py:60
  311.3 2.8 broadcast_in_dim.9
  314.1 28.1 %scatter_fusion = bf16[4,4096,128]{2,0,1:T(4,128)(2,1)} fusion(bf16[4,4096,128]{2,0,1:T(4,128)(2,1)} %broadcast_in_dim.9, s32[256]{0:T(256)S(1)} %bitcast.67, bf16[256,4,128]{2,1,0:T(4,128)(2,1)S(1)} %bitcast.65), kind=kCustom, calls=%fused_computation.4 | custom fusion | bytes 787456 | tf_op jit(solution)/shard_map/scatter | solution.py:62
  342.1 4.7 copy.37
  346.8 7.1 %reshape.237 = bf16[4,2,1024,256]{3,2,1,0:T(8,128)(2,1)} reshape(bf16[4,4096,128]{2,1,0:T(8,128)(2,1)} %copy.37) | data formatting | bytes 8388608 | tf_op jit(solution)/shard_map/reshape | solution.py:63
  353.9 23.8 %convert_bitcast_fusion = bf16[4,2,1024,256]{2,3,1,0:T(8,128)(2,1)} fusion(bf16[4,2,1024,256]{3,2,1,0:T(8,128)(2,1)} %reshape.237), kind=kOutput, calls=%fused_computation.28 | convolution fusion | flops 4314890240 | bytes 8388608 | tf_op jit(solution)/shard_map/ya,mlac->mlyc/dot_general | solution.py:27
  377.6 11.1 %copy.39 = bf16[4,2,1024,256]{3,1,0,2:T(2,128)(2,1)} copy(bf16[4,2,1024,256]{2,3,1,0:T(8,128)(2,1)} %convert_bitcast_fusion) | data formatting | bytes 8388608 | tf_op jit(solution)/shard_map/convert_element_type | solution.py:28
  388.8 4.8 all-to-all-start.3
  393.6 68.2 %fusion.75 = bf16[2048,2048,1,1]{1,0,3,2:T(8,128)(2,1)} fusion(), kind=kLoop, calls=%fused_computation.16.clone.clone.clone.1 | loop fusion | flops 71303168 | bytes 8388608 | tf_op jit(solution)/shard_map/dot_general | solution.py:65
  461.8 25.8 %all-to-all-done.3 = bf16[4,2,1024,256]{3,1,0,2:T(2,128)(2,1)} async-done(((bf16[4,2,1024,256]{3,1,0,2:T(2,128)(2,1)}), bf16[4,2,1024,256]{3,1,0,2:T(2,128)(2,1)}, u32[]{:S(2)}, u32[]{:S(2)}) %all-to-all-start.3) | async-done | bytes 4194336 | tf_op jit(solution)/shard_map/all_to_all | solution.py:64
  487.6 6.6 %copy.46 = bf16[4,2,8,128,256]{4,2,3,1,0:T(8,128)(2,1)} copy(bf16[4,2,8,128,256]{4,1,0,3,2:T(2,128)(2,1)} %bitcast.14) | data formatting | bytes 8388608 | tf_op jit(solution)/shard_map/all_to_all | solution.py:64
  494.1 7.4 %dot_general.17 = bf16[4,2,128,2048]{3,2,1,0:T(8,128)(2,1)} reshape(bf16[4,2,128,8,256]{4,3,2,1,0:T(8,128)(2,1)} %bitcast.61) | data formatting | bytes 8388608 | tf_op jit(solution)/shard_map/dot_general | solution.py:65
  501.6 14.5 %fusion.9 = f32[4,2,128,2048]{3,2,1,0:T(8,128)} fusion(bf16[4,2,128,2048]{3,2,1,0:T(8,128)(2,1)} %dot_general.17, f32[2,128,2048]{2,1,0:T(8,128)S(1)} %broadcast_multiply_fusion, bf16[2048,2048,1,1]{1,0,3,2:T(8,128)(2,1)} %fusion.75), kind=kOutput, calls=%fused_computation.22 | convolution fusion | flops 8592031744 | bytes 23068672 | tf_op jit(solution)/shard_map/dot_general | solution.py:65
  (8 shorter events, 0.1 us)
Async XLA Ops:
  0.0 68.2 %copy-start.2 = (f32[2,2048]{1,0:T(2,128)S(1)}, f32[2,2048]{1,0:T(2,128)}, u32[]{:S(2)}) copy-start(f32[2,2048]{1,0:T(2,128)} %param.10) | copy-start | bytes 49156
  0.0 68.2 %copy-start.5 = (f32[2,128]{1,0:T(2,128)S(1)}, f32[2,128]{1,0:T(2,128)}, u32[]{:S(2)}) copy-start(f32[2,128]{1,0:T(2,128)} %param.9) | copy-start | bytes 3076
  0.0 68.4 %copy-start = (f32[4,2,128,2048]{3,2,1,0:T(8,128)S(1)}, f32[4,2,128,2048]{3,2,1,0:T(8,128)}, u32[]{:S(2)}) copy-start(f32[4,2,128,2048]{3,2,1,0:T(8,128)} %param.7) | copy-start | bytes 25165828
  93.6 6.5 %copy-start.3 = (s32[256]{0:T(256)S(1)}, s32[256]{0:T(256)}, u32[]{:S(2)}) copy-start(s32[256]{0:T(256)} %param.11) | copy-start | bytes 3076
  93.6 100.6 %all-to-all-start = ((bf16[4,2,128,2048]{2,1,0,3:T(2,128)(2,1)}), bf16[4,2,128,2048]{2,1,0,3:T(2,128)(2,1)}, u32[]{:S(2)}, u32[]{:S(2)}) async-start(bf16[4,2,128,2048]{2,1,0,3:T(2,128)(2,1)} %copy.33), calls=%async_computation | async-start | bytes 8388608 | tf_op jit(solution)/shard_map/all_to_all | solution.py:34
  256.4 24.4 %all-to-all-start.1 = ((bf16[4,256,128]{2,0,1:T(4,128)(2,1)}), bf16[4,256,128]{2,0,1:T(4,128)(2,1)S(1)}, u32[]{:S(2)}, u32[]{:S(2)}) async-start(bf16[4,256,128]{2,0,1:T(4,128)(2,1)} %bitcast.10), calls=%async_computation.1 | async-start | bytes 524288 | tf_op jit(solution)/shard_map/all_to_all | solution.py:51
  270.0 21.9 %copy-start.1 = (f32[256,128]{1,0:T(8,128)S(1)}, f32[256,128]{1,0:T(8,128)}, u32[]{:S(2)}) copy-start(f32[256,128]{1,0:T(8,128)} %param.13) | copy-start | bytes 393220
  270.0 21.9 %copy-start.4 = (s32[256]{0:T(256)S(1)}, s32[256]{0:T(256)}, u32[]{:S(2)}) copy-start(s32[256]{0:T(256)} %param.12) | copy-start | bytes 3076
  388.8 98.8 %all-to-all-start.3 = ((bf16[4,2,1024,256]{3,1,0,2:T(2,128)(2,1)}), bf16[4,2,1024,256]{3,1,0,2:T(2,128)(2,1)}, u32[]{:S(2)}, u32[]{:S(2)}) async-start(bf16[4,2,1024,256]{3,1,0,2:T(2,128)(2,1)} %copy.39), calls=%async_computation.3 | async-start | bytes 8388608 | tf_op jit(solution)/shard_map/all_to_all | solution.py:64
